TPU v7x, 32 devices: a whole 2x2x4 slice. The times are simulated.
32 devices in a mesh: rows: 8 (over z, x), strips: 4 (over y, core).
Axes of the slice: x: 2, y: 2, z: 4, core: 2. Of those that a mesh axis runs over, the one named last changes fastest.
Arguments:
- tokens: bfloat16 [8, 24, 64, 1280], P('rows', None, 'strips'), may hold values from -8 to 8
- stale_kv: bfloat16 [8, 2, 1536, 1280], P('rows', None, 'strips'), may hold values from -180 to 180
- stale_moments: float32 [8, 4, 2, 32], P('rows', 'strips'), as said below
- norm_gain: float32 [1280], replicated, may hold values from 0.1 to 1.9
- norm_bias: float32 [1280], replicated, may hold values from -3 to 3
- w_query: bfloat16 [1280, 1280], P('rows'), may hold values from -0.33398438 to 0.33398438
- w_key: bfloat16 [1280, 1280], P('rows'), may hold values from -0.1953125 to 0.1953125
- w_value: bfloat16 [1280, 1280], P('rows'), may hold values from -0.15625 to 0.15625
- w_out: bfloat16 [1280, 1280], P('rows'), may hold values from -0.33398438 to 0.33398438
Outputs:
- attended: bfloat16 [8, 24, 64, 1280], P('rows', None, 'strips')
- fresh_kv: bfloat16 [8, 2, 1536, 1280], P('rows', None, 'strips')
- fresh_sums: float32 [8, 4, 32], P('rows', 'strips')
- fresh_squares: float32 [8, 4, 32], P('rows', 'strips')
Inputs may be any that keep to these rules, and one draw needn't show every extreme that they name: `stale_moments`: each strip's entries are a sum of 15360 values and the sum of their squares.
All inputs are finite; a program needn't handle non-finite values.
Results may differ from a plain program's by a relative error of at most 0.0075.
The roundings to bfloat16 on the way count: a program that leaves them out, or rounds other values in their place, can miss the bound.
Values may be sent and summed in bfloat16 or wider, within the bound.
No kernel may reach another device: no remote copies, remote signals or barrier semaphores. Data moves between devices by JAX's collectives and lax.ppermute only.
A program may use at most 128 MiB of HBM per device.

v0:
```python
import jax
import jax.numpy as jnp
from jax import lax
from jax.sharding import PartitionSpec as P

HEADS = 20
HEAD = 64


def fold_keys(carry, piece, query_heads, own_start, own_count):
    top_score, total, weighted = carry
    count = piece.shape[1]
    heads = query_heads.shape[0]
    size = query_heads.shape[2]
    keys_part = piece[0].reshape(count, heads, size).transpose(1, 0, 2)
    vals_part = piece[1].reshape(count, heads, size).transpose(1, 0, 2)
    places = jnp.arange(count, dtype=jnp.int32)
    inside = (places >= own_start) & (places < own_start + own_count)

    def per_head(items):
        head_top, head_total, head_sum, head_query, head_keys, head_vals = items
        scores = jnp.dot(head_query, head_keys.T, preferred_element_type=jnp.float32)
        scores = jnp.where(inside[None, :], jnp.float32(-1e30), scores)
        new_top = jnp.maximum(head_top, scores.max(axis=-1))
        factor = jnp.exp(head_top - new_top)
        weights = jnp.exp(scores - new_top[:, None])
        upper = weights.astype(jnp.bfloat16)
        lower = (weights - upper.astype(jnp.float32)).astype(jnp.bfloat16)
        head_total = head_total * factor + weights.sum(axis=-1)
        product = jnp.dot(upper, head_vals, preferred_element_type=jnp.float32) + jnp.dot(
            lower, head_vals, preferred_element_type=jnp.float32
        )
        head_sum = head_sum * factor[:, None] + product
        return (new_top, head_total, head_sum)

    return lax.map(per_head, (top_score, total, weighted, query_heads, keys_part, vals_part))


def shards(tokens, stale_kv, stale_moments, norm_gain, norm_bias, w_query, w_key, w_value, w_out):
    band, width, chans = (tokens.shape[1], tokens.shape[2], tokens.shape[3])
    tok_count = band * width
    groups = stale_moments.shape[3]
    per_group = chans // groups
    strips = lax.axis_size("strips")
    flat = tokens.reshape(tok_count, chans).astype(jnp.float32)
    grouped = flat.reshape(tok_count, groups, per_group)
    fresh = jnp.stack([grouped.sum(axis=(0, 2)), (grouped * grouped).sum(axis=(0, 2))])
    own_moments = stale_moments[0]
    own_kv = stale_kv[0]
    totals = lax.psum(own_moments[0], "strips")
    mixed = totals - own_moments[0] + fresh
    count = float(tok_count * strips * per_group)
    mean = mixed[0] / count
    var = mixed[1] / count - mean * mean
    rstd = lax.rsqrt(var + 1e-05)
    normed = ((grouped - mean[None, :, None]) * rstd[None, :, None]).reshape(tok_count, chans)
    normed = (normed * norm_gain + norm_bias).astype(jnp.bfloat16)
    strip_index = lax.axis_index("strips")
    pieces = (
        lax.all_gather(w_query, "rows", axis=0, tiled=True),
        lax.all_gather(w_key, "rows", axis=0, tiled=True),
        lax.all_gather(w_value, "rows", axis=0, tiled=True),
    )
    columns = normed
    query_sum, key_sum, value_sum = tuple(
        (jnp.dot(columns, piece, preferred_element_type=jnp.float32) for piece in pieces)
    )
    query = (query_sum * (1.0 / HEAD**0.5)).astype(jnp.bfloat16)
    key = key_sum.astype(jnp.bfloat16)
    value = value_sum.astype(jnp.bfloat16)
    fresh_kv = jnp.stack([key, value])
    query_heads = query.reshape(tok_count, HEADS, HEAD).transpose(1, 0, 2)
    start_carry = (
        jnp.full((HEADS, tok_count), -1e30, jnp.float32),
        jnp.zeros((HEADS, tok_count), jnp.float32),
        jnp.zeros((HEADS, tok_count, HEAD), jnp.float32),
    )
    carry = fold_keys(start_carry, fresh_kv, query_heads, 0, 0)
    own_start = strip_index * tok_count
    top_score, total, weighted = fold_keys(
        carry,
        lax.all_gather(own_kv, "strips", axis=1, tiled=True),
        query_heads,
        own_start,
        tok_count,
    )
    heads_out = (
        (weighted / total[..., None])
        .transpose(1, 0, 2)
        .reshape(tok_count, HEADS * HEAD)
        .astype(jnp.bfloat16)
    )
    columns = heads_out
    attended = jnp.dot(
        columns,
        lax.all_gather(w_out, "rows", axis=0, tiled=True),
        preferred_element_type=jnp.float32,
    )
    attended = attended.astype(jnp.bfloat16)
    return (
        attended.reshape(1, band, width, chans),
        fresh_kv[None],
        fresh[0][None, None],
        fresh[1][None, None],
    )


def solution(mesh):
    in_specs = (
        P("rows", None, "strips", None),
        P("rows", None, "strips", None),
        P("rows", "strips", None, None),
        P(),
        P(),
        P("rows", None),
        P("rows", None),
        P("rows", None),
        P("rows", None),
    )
    out_specs = (
        P("rows", None, "strips", None),
        P("rows", None, "strips", None),
        P("rows", "strips", None),
        P("rows", "strips", None),
    )
    return jax.shard_map(shards, mesh=mesh, in_specs=in_specs, out_specs=out_specs, check_vma=False)
```

profile of v0, /device:TPU:0, one launch (start us, length us, event | category | flops | bytes accessed | tf_op | source)
XLA Modules:
  0.0 416.8 jit_solution(2687440719954865516)
XLA Ops:
  9.4 4.0 copy.32
  15.1 8.4 %psum.7 = f32[2,32]{1,0:T(2,128)S(1)} all-reduce(f32[2,32]{1,0:T(2,128)S(1)} %bitcast.135), channel_id=1, replica_groups=mesh['rows'=8,'strips'=4] {'strips'}, use_global_device_ids=true, to_apply=%region_0.0 | all-reduce | flops 64 | bytes 512 | tf_op jit(solution)/shard_map/psum | solution.py:50
  24.5 49.8 %all-gather.7.cloned.1.call-done = bf16[1280,1280]{1,0:T(8,128)(2,1)} async-done(((bf16[160,1280]{1,0:T(8,128)(2,1)}), bf16[1280,1280]{1,0:T(8,128)(2,1)}) %all-gather.7.cloned.1.call-update) | async-done | bytes 3276816 | tf_op jit(solution)/shard_map/all_gather | solution.py:60
  74.4 3.4 fusion.49
  79.5 57.2 %all-gather.9.cloned.1.call-done = bf16[1280,1280]{1,0:T(8,128)(2,1)} async-done(((bf16[160,1280]{1,0:T(8,128)(2,1)}), bf16[1280,1280]{1,0:T(8,128)(2,1)}) %all-gather.9.cloned.1.call-update) | async-done | bytes 3276816 | tf_op jit(solution)/shard_map/all_gather | solution.py:61
  136.7 3.7 convolution_convert_fusion.2
  141.7 57.4 %all-gather.11.cloned.1.call-done = bf16[1280,1280]{1,0:T(8,128)(2,1)} async-done(((bf16[160,1280]{1,0:T(8,128)(2,1)}), bf16[1280,1280]{1,0:T(8,128)(2,1)}) %all-gather.11.cloned.1.call-update) | async-done | bytes 3276816 | tf_op jit(solution)/shard_map/all_gather | solution.py:62
  199.1 4.7 %convolution_convert_fusion.1 = bf16[384,1280]{1,0:T(8,128)(2,1)} fusion(bf16[384,1280]{1,0:T(8,128)(2,1)} %copy-done.2, bf16[1280,1280]{1,0:T(8,128)(2,1)} %all-gather.11.cloned.1.call-done), kind=kOutput, calls=%fused_computation.65 | convolution fusion | flops 1258782720 | bytes 5242880 | tf_op jit(solution)/shard_map/dot_general | solution.py:66
  203.7 2.2 copy.28
  206.0 1.5 broadcast.114.clone
  207.5 82.3 %while.28 = (s32[]{:T(128)}, f32[20,384]{1,0:T(8,128)S(1)}, f32[20,384]{1,0:T(8,128)S(1)}, f32[20,384,64]{1,2,0:T(8,128)}, bf16[20,384,64]{2,1,0:T(8,128)(2,1)S(...) while((s32[]{:T(128)}, f32[20,384]{1,0:T(8,128)S(1)}, ...), condition=%wide.region_8.9_spmd, body=%wide.region_5.8_spmd.sunk | while | flops 58148352 | bytes 2930277 | solution.py:36
  209.7 1.7 fusion.90
  213.8 1.7 fusion.90
  217.9 1.7 fusion.90
  222.0 1.7 fusion.90
  226.1 1.7 fusion.90
  230.2 1.7 fusion.90
  234.4 1.7 fusion.90
  238.5 1.7 fusion.90
  242.6 1.7 fusion.90
  246.7 1.7 fusion.90
  250.8 1.7 fusion.90
  254.9 1.7 fusion.90
  259.0 1.7 fusion.90
  263.2 1.7 fusion.90
  267.3 1.7 fusion.90
  271.4 1.7 fusion.90
  275.5 1.7 fusion.90
  279.6 1.7 fusion.90
  283.8 1.7 fusion.90
  287.9 1.7 fusion.90
  289.9 3.4 maximum_bitcast_fusion
  293.2 5.6 %fusion.58 = (bf16[1,1,1536,1280]{2,3,1,0:T(8,128)(2,1)}, bf16[1,1,1536,1280]{2,3,1,0:T(8,128)(2,1)}) fusion(bf16[1,2,1536,1280]{2,3,1,0:T(8,128)(2,1)} %all-gather.15.cloned.1.call-done), kind=kLoop, calls=%fused_computation.83 | loop fusion | bytes 15728640 | tf_op jit(solution)/shard_map/slice | solution.py:16
  299.0 106.6 %while.29 = (s32[]{:T(128)}, f32[20,384]{1,0:T(8,128)S(1)}, f32[20,384,64]{1,2,0:T(8,128)S(1)}, f32[20,384]{1,0:T(8,128)S(1)}, f32[20,384]{1,0:T(8,128)S(1)}, /*...) while((s32[]{:T(128)}, f32[20,384]{1,0:T(8,128)S(1)}, ...), condition=%wide.region_12.13_spmd.clone, body=%wide.region_9.12_spmd.clone.sunk | while | flops 233060352 | bytes 10554513 | solution.py:36
  300.6 1.5 fusion.99
  302.2 1.6 fusion.100
  307.5 1.6 fusion.100
  311.3 1.5 fusion.99
  312.8 1.6 fusion.100
  318.2 1.6 fusion.100
  321.9 1.5 fusion.99
  323.5 1.6 fusion.100
  327.3 1.5 fusion.99
  328.8 1.6 fusion.100
  332.6 1.5 fusion.99
  334.2 1.6 fusion.100
  337.9 1.5 fusion.99
  339.5 1.6 fusion.100
  343.3 1.5 fusion.99
  344.8 1.6 fusion.100
  348.6 1.5 fusion.99
  350.2 1.6 fusion.100
  353.9 1.5 fusion.99
  355.5 1.6 fusion.100
  360.8 1.6 fusion.100
  366.1 1.6 fusion.100
  371.5 1.6 fusion.100
  376.8 1.6 fusion.100
  382.1 1.6 fusion.100
  387.5 1.6 fusion.100
  392.8 1.6 fusion.100
  398.1 1.6 fusion.100
  403.5 1.6 fusion.100
  405.9 4.4 %convolution_convert_fusion = bf16[384,1280]{1,0:T(8,128)(2,1)} fusion(bf16[384,1280]{0,1:T(8,128)(2,1)S(1)} %bitcast.134, bf16[1280,1280]{1,0:T(8,128)(2,1)} %all-gather.13.cloned.1.call-done), kind=kOutput, calls=%fused_computation.64 | convolution fusion | flops 1258782720 | bytes 5242880 | tf_op jit(solution)/shard_map/dot_general | solution.py:94
  (360 shorter events, 114.8 us)
Async XLA Ops:
  7.2 67.2 %all-gather.7.cloned.1.call-start = ((), (), s32[]{:S(2)}) async-start(), calls=%async_computation | async-start | bytes 3686400 | tf_op jit(solution)/shard_map/all_gather | solution.py:60
  7.9 128.8 %all-gather.9.cloned.1.call-start = ((), (), s32[]{:S(2)}) async-start(), calls=%async_computation.1 | async-start | bytes 3686400 | tf_op jit(solution)/shard_map/all_gather | solution.py:61
  8.6 190.4 %all-gather.11.cloned.1.call-start = ((), (), s32[]{:S(2)}) async-start(), calls=%async_computation.2 | async-start | bytes 3686400 | tf_op jit(solution)/shard_map/all_gather | solution.py:62
  9.4 283.9 %all-gather.15.cloned.1.call-start = ((), (), s32[]{:S(2)}) async-start(), calls=%async_computation.4 | async-start | bytes 9830400 | tf_op jit(solution)/shard_map/all_gather | solution.py:82
  13.4 1.2 copy-start.1
  13.4 1.7 copy-start.5
  13.4 10.7 %copy-start.3 = (f32[1280]{0:T(1024)S(1)}, f32[1280]{0:T(1024)}, u32[]{:S(2)}) copy-start(f32[1280]{0:T(1024)} %param.17) | copy-start | bytes 15364
  13.4 10.7 %copy-start.4 = (f32[1280]{0:T(1024)S(1)}, f32[1280]{0:T(1024)}, u32[]{:S(2)}) copy-start(f32[1280]{0:T(1024)} %param.16) | copy-start | bytes 15364
  13.5 392.4 %all-gather.13.cloned.1.call-start = ((), (), s32[]{:S(2)}) async-start(), calls=%async_computation.3 | async-start | bytes 3686400 | tf_op jit(solution)/shard_map/all_gather | solution.py:96
  23.6 54.1 %copy-start.6 = (f32[32]{0:T(128)}, f32[32]{0:T(128)S(1)}, u32[]{:S(2)}) copy-start(f32[32]{0:T(128)S(1)} %reduce_sum.58) | copy-start | bytes 388
  23.7 54.0 %copy-start.7 = (f32[32]{0:T(128)}, f32[32]{0:T(128)S(1)}, u32[]{:S(2)}) copy-start(f32[32]{0:T(128)S(1)} %reduce_sum.61) | copy-start | bytes 388
  24.5 53.2 %copy-start.2 = (bf16[384,1280]{1,0:T(8,128)(2,1)}, bf16[384,1280]{1,0:T(8,128)(2,1)S(1)}, u32[]{:S(2)}) copy-start(bf16[384,1280]{1,0:T(8,128)(2,1)S(1)} %fusion.53) | copy-start | bytes 2949124
  289.9 3.4 copy-start
Sparse Core Ops, SparseCore 0:
  10.2 64.1 all-gather.6
  76.5 60.1 all-gather.8
  138.9 60.1 all-gather.10
  200.5 53.8 all-gather.14
  256.4 61.4 all-gather.12
where the time goes:
time: 422 us; the launch traced here: 417 us
  matrix products  186 us (44%)
  waiting for transfers between devices  167 us (40%)
  local copies, waits for them, and re-layouts  21.4 us (5%)
  other arithmetic  17.5 us (4%)
  between operations  14 us (3%)
  blocking collectives  8.4 us (2%)
    dot_general x40, matrix products, per_head(): jnp.dot(lower, head_vals, preferred_element_type=jnp.float32)  66.4 us
    all_gather x1, waiting for transfers between devices, shards(): lax.all_gather(w_value, 'rows', axis=0, tiled=True)  57.4 us
    all_gather x1, waiting for transfers between devices, shards(): lax.all_gather(w_key, 'rows', axis=0, tiled=True)  57.2 us
    dot_general x40, matrix products, per_head(): jnp.dot(head_query, head_keys.T, preferred_element_type=jnp.float32)  52.4 us
    dot_general x40, matrix products, per_head(): jnp.dot(upper, head_vals, preferred_element_type=jnp.float32)  51.4 us
    all_gather x1, waiting for transfers between devices, shards(): lax.all_gather(w_query, 'rows', axis=0, tiled=True)  49.8 us
    reduce_sum x40, other arithmetic, per_head(): head_total = head_total * factor + weights.sum(axis=-1)  11.8 us
    dot_general x3, matrix products, shards(): jnp.dot(columns, piece, preferred_element_type=jnp.float32)  11.7 us
  transfers between devices with their start and end apart: 5, of which 3 were waited for; matrix products, arithmetic and copies ran while one was open for 53% of the time, Pallas kernels for 0%

commit v1 on v0

--- a/solution.py
+++ b/solution.py
@@ -56,9 +56,23 @@
     normed = ((grouped - mean[None, :, None]) * rstd[None, :, None]).reshape(tok_count, chans)
     normed = (normed * norm_gain + norm_bias).astype(jnp.bfloat16)
     strip_index = lax.axis_index("strips")
+
+    def plan_arrays(load, device_axis, out_dim=0):
+        runs = [load]
+        ndev = lax.axis_size(device_axis)
+        for p in range(1, ndev):
+            left_arr = lax.ppermute(
+                runs[p - 1], axis_name=device_axis, perm=[(m, (m - 1) % ndev) for m in range(ndev)]
+            )
+            runs.append(left_arr)
+        step_out = jnp.concatenate(runs, axis=out_dim)
+        y = lax.axis_index(device_axis)
+        passed = jnp.roll(step_out, y * load.shape[out_dim], axis=out_dim)
+        return passed
+
     pieces = (
         lax.all_gather(w_query, "rows", axis=0, tiled=True),
-        lax.all_gather(w_key, "rows", axis=0, tiled=True),
+        plan_arrays(w_key, "rows"),
         lax.all_gather(w_value, "rows", axis=0, tiled=True),
     )
     columns = normed

time: 422 us -> 400 us (0.948)
  waiting for transfers between devices: 167 us -> 114 us
  starting transfers between devices: 0.19 us -> 37.3 us
    ppermute x0 -> x7, waiting for transfers between devices: none -> 81.5 us  [plan_arrays(): lax.ppermute(runs[p - 1], axis_name=device_axis, perm=[(m, (m - 1) % ndev...]
    all_gather x1 -> x0, waiting for transfers between devices: 57.2 us -> none  [shards(): lax.all_gather(w_key, 'rows', axis=0, tiled=True)]
    all_gather x1, waiting for transfers between devices: 49.8 us -> 0.01 us  [shards(): lax.all_gather(w_query, 'rows', axis=0, tiled=True)]
    ppermute x0 -> x7, starting transfers between devices: none -> 37.1 us  [plan_arrays(): lax.ppermute(runs[p - 1], axis_name=device_axis, perm=[(m, (m - 1) % ndev...]
    all_gather x1, waiting for transfers between devices: 57.4 us -> 31 us  [shards(): lax.all_gather(w_value, 'rows', axis=0, tiled=True)]
  transfers between devices with their start and end apart: 5 -> 11, of which waited for: 3 -> 8; matrix products, arithmetic and copies ran while one was open for 53% -> 55% of each run, Pallas kernels for 0% -> 0%
where the time goes in v1:
time: 400 us; the launch traced here: 396 us
  matrix products  183 us (46%)
  waiting for transfers between devices  114 us (28%)
  starting transfers between devices  37.3 us (9%)
  local copies, waits for them, and re-layouts  20.5 us (5%)
  other arithmetic  17.5 us (4%)
  between operations  14.2 us (4%)
  blocking collectives  6.63 us (2%)
    ppermute x7, waiting for transfers between devices, plan_arrays(): lax.ppermute(runs[p - 1], axis_name=device_axis, perm=[(m, (m - 1) % ndev...  81.5 us
    dot_general x40, matrix products, per_head(): jnp.dot(lower, head_vals, preferred_element_type=jnp.float32)  66.4 us
    dot_general x40, matrix products, per_head(): jnp.dot(head_query, head_keys.T, preferred_element_type=jnp.float32)  52.4 us
    dot_general x40, matrix products, per_head(): jnp.dot(upper, head_vals, preferred_element_type=jnp.float32)  51.4 us
    ppermute x7, starting transfers between devices, plan_arrays(): lax.ppermute(runs[p - 1], axis_name=device_axis, perm=[(m, (m - 1) % ndev...  37.1 us
    all_gather x1, waiting for transfers between devices, shards(): lax.all_gather(w_value, 'rows', axis=0, tiled=True)  31 us
    reduce_sum x40, other arithmetic, per_head(): head_total = head_total * factor + weights.sum(axis=-1)  11.8 us
    dot_general x3, matrix products, shards(): jnp.dot(columns, piece, preferred_element_type=jnp.float32)  8.82 us
  transfers between devices with their start and end apart: 11, of which 8 were waited for; matrix products, arithmetic and copies ran while one was open for 55% of the time, Pallas kernels for 0%

profile of v1, /device:TPU:0, one launch (start us, length us, event | category | flops | bytes accessed | tf_op | source)
XLA Modules:
  0.0 395.5 jit_solution(3391208759953531299)
XLA Ops:
  8.7 4.1 %copy.32 = bf16[1,2,384,1280]{2,3,1,0:T(8,128)(2,1)} copy(bf16[1,2,384,1280]{3,2,1,0:T(8,128)(2,1)} %param.14) | data formatting | bytes 3932160 | tf_op args[1]
  12.9 6.1 %collective-permute-start = (bf16[160,1280]{1,0:T(8,128)(2,1)S(1)}, bf16[160,1280]{1,0:T(8,128)(2,1)S(1)}, u32[]{:S(2)}, u32[]{:S(2)}) collective-permute-start(bf16[160,1280]{1,0:T(8,128)(2,1)S(1)} %copy-done.5), channel_id=1, source_target_pairs={{0,28},{4,0},{8,4},{12,8},{16,12},{20,16},{24,20},{28,24},{1,29},{... | collective-permute-start | bytes 1228808 | tf_op jit(solution)/shard_map/ppermute | solution.py:64
  19.8 6.6 %psum.7 = f32[2,32]{1,0:T(2,128)S(1)} all-reduce(f32[2,32]{1,0:T(2,128)S(1)} %bitcast.134), channel_id=1, replica_groups=mesh['rows'=8,'strips'=4] {'strips'}, use_global_device_ids=true, to_apply=%region_0.0 | all-reduce | flops 64 | bytes 512 | tf_op jit(solution)/shard_map/psum | solution.py:50
  26.4 8.4 %collective-permute-done = bf16[160,1280]{1,0:T(8,128)(2,1)S(1)} collective-permute-done((bf16[160,1280]{1,0:T(8,128)(2,1)S(1)}, bf16[160,1280]{1,0:T(8,128)(2,1)S(1)}, u32[]{:S(2)}, u32[]{:S(2)}) %collective-permute-start) | collective-permute-done | bytes 409632 | tf_op jit(solution)/shard_map/ppermute | solution.py:64
  34.8 5.2 %collective-permute-start.1 = (bf16[160,1280]{1,0:T(8,128)(2,1)S(1)}, bf16[160,1280]{1,0:T(8,128)(2,1)S(1)}, u32[]{:S(2)}, u32[]{:S(2)}) collective-permute-start(bf16[160,1280]{1,0:T(8,128)(2,1)S(1)} %collective-permute-done), channel_id=1, source_target_pairs={{0,28},{4,0},{8,4},{12,8},{16,12},{20,16},{24,20},{28,24},{1,29},{... | collective-permute-start | bytes 1228808 | tf_op jit(solution)/shard_map/ppermute | solution.py:64
  40.2 9.4 %collective-permute-done.1 = bf16[160,1280]{1,0:T(8,128)(2,1)S(1)} collective-permute-done((bf16[160,1280]{1,0:T(8,128)(2,1)S(1)}, bf16[160,1280]{1,0:T(8,128)(2,1)S(1)}, u32[]{:S(2)}, u32[]{:S(2)}) %collective-permute-start.1) | collective-permute-done | bytes 409632 | tf_op jit(solution)/shard_map/ppermute | solution.py:64
  49.7 5.2 %collective-permute-start.2 = (bf16[160,1280]{1,0:T(8,128)(2,1)S(1)}, bf16[160,1280]{1,0:T(8,128)(2,1)S(1)}, u32[]{:S(2)}, u32[]{:S(2)}) collective-permute-start(bf16[160,1280]{1,0:T(8,128)(2,1)S(1)} %collective-permute-done.1), channel_id=1, source_target_pairs={{0,28},{4,0},{8,4},{12,8},{16,12},{20,16},{24,20},{28,24},{1,29},{... | collective-permute-start | bytes 1228808 | tf_op jit(solution)/shard_map/ppermute | solution.py:64
  55.1 16.3 %collective-permute-done.2 = bf16[160,1280]{1,0:T(8,128)(2,1)S(1)} collective-permute-done((bf16[160,1280]{1,0:T(8,128)(2,1)S(1)}, bf16[160,1280]{1,0:T(8,128)(2,1)S(1)}, u32[]{:S(2)}, u32[]{:S(2)}) %collective-permute-start.2) | collective-permute-done | bytes 409632 | tf_op jit(solution)/shard_map/ppermute | solution.py:64
  71.3 5.2 %collective-permute-start.3 = (bf16[160,1280]{1,0:T(8,128)(2,1)S(1)}, bf16[160,1280]{1,0:T(8,128)(2,1)S(1)}, u32[]{:S(2)}, u32[]{:S(2)}) collective-permute-start(bf16[160,1280]{1,0:T(8,128)(2,1)S(1)} %collective-permute-done.2), channel_id=1, source_target_pairs={{0,28},{4,0},{8,4},{12,8},{16,12},{20,16},{24,20},{28,24},{1,29},{... | collective-permute-start | bytes 1228808 | tf_op jit(solution)/shard_map/ppermute | solution.py:64
  76.9 16.5 %collective-permute-done.3 = bf16[160,1280]{1,0:T(8,128)(2,1)S(1)} collective-permute-done((bf16[160,1280]{1,0:T(8,128)(2,1)S(1)}, bf16[160,1280]{1,0:T(8,128)(2,1)S(1)}, u32[]{:S(2)}, u32[]{:S(2)}) %collective-permute-start.3) | collective-permute-done | bytes 409632 | tf_op jit(solution)/shard_map/ppermute | solution.py:64
  93.4 5.2 %collective-permute-start.4 = (bf16[160,1280]{1,0:T(8,128)(2,1)S(1)}, bf16[160,1280]{1,0:T(8,128)(2,1)S(1)}, u32[]{:S(2)}, u32[]{:S(2)}) collective-permute-start(bf16[160,1280]{1,0:T(8,128)(2,1)S(1)} %collective-permute-done.3), channel_id=1, source_target_pairs={{0,28},{4,0},{8,4},{12,8},{16,12},{20,16},{24,20},{28,24},{1,29},{... | collective-permute-start | bytes 1228808 | tf_op jit(solution)/shard_map/ppermute | solution.py:64
  98.6 7.8 %collective-permute-done.4 = bf16[160,1280]{1,0:T(8,128)(2,1)S(1)} collective-permute-done((bf16[160,1280]{1,0:T(8,128)(2,1)S(1)}, bf16[160,1280]{1,0:T(8,128)(2,1)S(1)}, u32[]{:S(2)}, u32[]{:S(2)}) %collective-permute-start.4) | collective-permute-done | bytes 409632 | tf_op jit(solution)/shard_map/ppermute | solution.py:64
  106.4 5.2 %collective-permute-start.5 = (bf16[160,1280]{1,0:T(8,128)(2,1)S(1)}, bf16[160,1280]{1,0:T(8,128)(2,1)S(1)}, u32[]{:S(2)}, u32[]{:S(2)}) collective-permute-start(bf16[160,1280]{1,0:T(8,128)(2,1)S(1)} %collective-permute-done.4), channel_id=1, source_target_pairs={{0,28},{4,0},{8,4},{12,8},{16,12},{20,16},{24,20},{28,24},{1,29},{... | collective-permute-start | bytes 1228808 | tf_op jit(solution)/shard_map/ppermute | solution.py:64
  111.6 6.1 %collective-permute-done.5 = bf16[160,1280]{1,0:T(8,128)(2,1)S(1)} collective-permute-done((bf16[160,1280]{1,0:T(8,128)(2,1)S(1)}, bf16[160,1280]{1,0:T(8,128)(2,1)S(1)}, u32[]{:S(2)}, u32[]{:S(2)}) %collective-permute-start.5) | collective-permute-done | bytes 409632 | tf_op jit(solution)/shard_map/ppermute | solution.py:64
  117.8 5.2 %collective-permute-start.6 = (bf16[160,1280]{1,0:T(8,128)(2,1)S(1)}, bf16[160,1280]{1,0:T(8,128)(2,1)S(1)}, u32[]{:S(2)}, u32[]{:S(2)}) collective-permute-start(bf16[160,1280]{1,0:T(8,128)(2,1)S(1)} %collective-permute-done.5), channel_id=1, source_target_pairs={{0,28},{4,0},{8,4},{12,8},{16,12},{20,16},{24,20},{28,24},{1,29},{... | collective-permute-start | bytes 1228808 | tf_op jit(solution)/shard_map/ppermute | solution.py:64
  123.0 17.0 %collective-permute-done.6 = bf16[160,1280]{1,0:T(8,128)(2,1)S(1)} collective-permute-done((bf16[160,1280]{1,0:T(8,128)(2,1)S(1)}, bf16[160,1280]{1,0:T(8,128)(2,1)S(1)}, u32[]{:S(2)}, u32[]{:S(2)}) %collective-permute-start.6) | collective-permute-done | bytes 409632 | tf_op jit(solution)/shard_map/ppermute | solution.py:64
  143.1 3.7 fusion.51
  148.6 31.0 %all-gather.8.cloned.1.call-done = bf16[1280,1280]{1,0:T(8,128)(2,1)} async-done(((bf16[160,1280]{1,0:T(8,128)(2,1)}), bf16[1280,1280]{1,0:T(8,128)(2,1)}) %all-gather.8.cloned.1.call-update) | async-done | bytes 3276816 | tf_op jit(solution)/shard_map/all_gather | solution.py:76
  179.5 3.7 convolution_convert_fusion.1
  186.1 82.5 %while.28 = (s32[]{:T(128)}, f32[20,384]{1,0:T(8,128)S(1)}, f32[20,384]{1,0:T(8,128)S(1)}, f32[20,384,64]{1,2,0:T(8,128)}, bf16[20,384,64]{2,1,0:T(8,128)(2,1)S(...) while((s32[]{:T(128)}, f32[20,384]{1,0:T(8,128)S(1)}, ...), condition=%wide.region_8.9_spmd, body=%wide.region_5.8_spmd.sunk | while | flops 58148352 | bytes 2930277 | solution.py:36
  188.4 1.7 fusion.95
  192.5 1.7 fusion.95
  196.6 1.7 fusion.95
  200.8 1.7 fusion.95
  204.9 1.7 fusion.95
  209.0 1.7 fusion.95
  213.1 1.7 fusion.95
  217.2 1.7 fusion.95
  221.3 1.7 fusion.95
  225.5 1.7 fusion.95
  229.6 1.7 fusion.95
  233.7 1.7 fusion.95
  237.8 1.7 fusion.95
  241.9 1.7 fusion.95
  246.0 1.7 fusion.95
  250.2 1.7 fusion.95
  254.3 1.7 fusion.95
  258.4 1.7 fusion.95
  262.5 1.7 fusion.95
  266.6 1.7 fusion.95
  268.6 3.4 maximum_bitcast_fusion
  272.0 5.6 %fusion.64 = (bf16[1,1,1536,1280]{2,3,1,0:T(8,128)(2,1)}, bf16[1,1,1536,1280]{2,3,1,0:T(8,128)(2,1)}) fusion(bf16[1,2,1536,1280]{2,3,1,0:T(8,128)(2,1)} %all-gather.12.cloned.1.call-done), kind=kLoop, calls=%fused_computation.102 | loop fusion | bytes 15728640 | tf_op jit(solution)/shard_map/slice | solution.py:16
  277.8 106.6 %while.29 = (s32[]{:T(128)}, f32[20,384]{1,0:T(8,128)S(1)}, f32[20,384,64]{1,2,0:T(8,128)S(1)}, f32[20,384]{1,0:T(8,128)S(1)}, f32[20,384]{1,0:T(8,128)S(1)}, /*...) while((s32[]{:T(128)}, f32[20,384]{1,0:T(8,128)S(1)}, ...), condition=%wide.region_12.13_spmd.clone, body=%wide.region_9.12_spmd.clone.sunk | while | flops 233060352 | bytes 10554513 | solution.py:36
  280.9 1.6 fusion.105
  286.2 1.6 fusion.105
  291.6 1.6 fusion.105
  296.9 1.6 fusion.105
  302.2 1.6 fusion.105
  307.5 1.6 fusion.105
  312.9 1.6 fusion.105
  318.2 1.6 fusion.105
  323.5 1.6 fusion.105
  328.9 1.6 fusion.105
  334.2 1.6 fusion.105
  339.5 1.6 fusion.105
  344.9 1.6 fusion.105
  350.2 1.6 fusion.105
  355.5 1.6 fusion.105
  360.9 1.6 fusion.105
  366.2 1.6 fusion.105
  371.5 1.6 fusion.105
  376.8 1.6 fusion.105
  382.2 1.6 fusion.105
  384.6 4.4 %convolution_convert_fusion = bf16[384,1280]{1,0:T(8,128)(2,1)} fusion(bf16[384,1280]{0,1:T(8,128)(2,1)S(1)} %bitcast.133, bf16[1280,1280]{1,0:T(8,128)(2,1)} %all-gather.10.cloned.1.call-done), kind=kOutput, calls=%fused_computation.67 | convolution fusion | flops 1258782720 | bytes 5242880 | tf_op jit(solution)/shard_map/dot_general | solution.py:108
  (395 shorter events, 131.8 us)
Async XLA Ops:
  7.2 5.8 %copy-start.5 = (bf16[160,1280]{1,0:T(8,128)(2,1)S(1)}, bf16[160,1280]{1,0:T(8,128)(2,1)}, u32[]{:S(2)}) copy-start(bf16[160,1280]{1,0:T(8,128)(2,1)} %param.19) | copy-start | bytes 1228804
  7.2 136.0 %all-gather.6.cloned.1.call-start = ((), (), s32[]{:S(2)}) async-start(), calls=%async_computation | async-start | bytes 3686400 | tf_op jit(solution)/shard_map/all_gather | solution.py:74
  7.9 11.1 %copy-start.1 = (bf16[1,24,16,1280]{3,2,1,0:T(8,128)(2,1)S(1)}, bf16[1,24,16,1280]{3,2,1,0:T(8,128)(2,1)}, u32[]{:S(2)}) copy-start(bf16[1,24,16,1280]{3,2,1,0:T(8,128)(2,1)} %param.13) | copy-start | bytes 2949124
  7.9 171.6 %all-gather.8.cloned.1.call-start = ((), (), s32[]{:S(2)}) async-start(), calls=%async_computation.1 | async-start | bytes 3686400 | tf_op jit(solution)/shard_map/all_gather | solution.py:76
  8.7 11.1 %copy-start.9 = (f32[1,1,2,32]{3,2,1,0:T(2,128)S(1)}, f32[1,1,2,32]{3,2,1,0:T(2,128)}, u32[]{:S(2)}) copy-start(f32[1,1,2,32]{3,2,1,0:T(2,128)} %param.15) | copy-start | bytes 772
  8.7 67.8 %copy-start.7 = (f32[1280]{0:T(1024)S(1)}, f32[1280]{0:T(1024)}, u32[]{:S(2)}) copy-start(f32[1280]{0:T(1024)} %param.17) | copy-start | bytes 15364
  8.7 67.8 %copy-start.8 = (f32[1280]{0:T(1024)S(1)}, f32[1280]{0:T(1024)}, u32[]{:S(2)}) copy-start(f32[1280]{0:T(1024)} %param.16) | copy-start | bytes 15364
  8.7 263.3 %all-gather.12.cloned.1.call-start = ((), (), s32[]{:S(2)}) async-start(), calls=%async_computation.3 | async-start | bytes 9830400 | tf_op jit(solution)/shard_map/all_gather | solution.py:96
  12.9 371.8 %all-gather.10.cloned.1.call-start = ((), (), s32[]{:S(2)}) async-start(), calls=%async_computation.2 | async-start | bytes 3686400 | tf_op jit(solution)/shard_map/all_gather | solution.py:110
  12.9 21.9 %collective-permute-start = (bf16[160,1280]{1,0:T(8,128)(2,1)S(1)}, bf16[160,1280]{1,0:T(8,128)(2,1)S(1)}, u32[]{:S(2)}, u32[]{:S(2)}) collective-permute-start(bf16[160,1280]{1,0:T(8,128)(2,1)S(1)} %copy-done.5), channel_id=1, source_target_pairs={{0,28},{4,0},{8,4},{12,8},{16,12},{20,16},{24,20},{28,24},{1,29},{... | collective-permute-start | bytes 1228808 | tf_op jit(solution)/shard_map/ppermute | solution.py:64
  19.6 103.3 %copy-start.10 = (f32[32]{0:T(128)}, f32[32]{0:T(128)S(1)}, u32[]{:S(2)}) copy-start(f32[32]{0:T(128)S(1)} %reduce_sum.58) | copy-start | bytes 388
  19.7 103.2 %copy-start.11 = (f32[32]{0:T(128)}, f32[32]{0:T(128)S(1)}, u32[]{:S(2)}) copy-start(f32[32]{0:T(128)S(1)} %reduce_sum.61) | copy-start | bytes 388
  34.8 14.8 %collective-permute-start.1 = (bf16[160,1280]{1,0:T(8,128)(2,1)S(1)}, bf16[160,1280]{1,0:T(8,128)(2,1)S(1)}, u32[]{:S(2)}, u32[]{:S(2)}) collective-permute-start(bf16[160,1280]{1,0:T(8,128)(2,1)S(1)} %collective-permute-done), channel_id=1, source_target_pairs={{0,28},{4,0},{8,4},{12,8},{16,12},{20,16},{24,20},{28,24},{1,29},{... | collective-permute-start | bytes 1228808 | tf_op jit(solution)/shard_map/ppermute | solution.py:64
  49.7 21.7 %collective-permute-start.2 = (bf16[160,1280]{1,0:T(8,128)(2,1)S(1)}, bf16[160,1280]{1,0:T(8,128)(2,1)S(1)}, u32[]{:S(2)}, u32[]{:S(2)}) collective-permute-start(bf16[160,1280]{1,0:T(8,128)(2,1)S(1)} %collective-permute-done.1), channel_id=1, source_target_pairs={{0,28},{4,0},{8,4},{12,8},{16,12},{20,16},{24,20},{28,24},{1,29},{... | collective-permute-start | bytes 1228808 | tf_op jit(solution)/shard_map/ppermute | solution.py:64
  71.3 22.0 %collective-permute-start.3 = (bf16[160,1280]{1,0:T(8,128)(2,1)S(1)}, bf16[160,1280]{1,0:T(8,128)(2,1)S(1)}, u32[]{:S(2)}, u32[]{:S(2)}) collective-permute-start(bf16[160,1280]{1,0:T(8,128)(2,1)S(1)} %collective-permute-done.2), channel_id=1, source_target_pairs={{0,28},{4,0},{8,4},{12,8},{16,12},{20,16},{24,20},{28,24},{1,29},{... | collective-permute-start | bytes 1228808 | tf_op jit(solution)/shard_map/ppermute | solution.py:64
  76.9 63.4 %copy-start.6 = (bf16[384,1280]{1,0:T(8,128)(2,1)}, bf16[384,1280]{1,0:T(8,128)(2,1)S(1)}, u32[]{:S(2)}) copy-start(bf16[384,1280]{1,0:T(8,128)(2,1)S(1)} %fusion.58) | copy-start | bytes 2949124
  93.4 13.0 %collective-permute-start.4 = (bf16[160,1280]{1,0:T(8,128)(2,1)S(1)}, bf16[160,1280]{1,0:T(8,128)(2,1)S(1)}, u32[]{:S(2)}, u32[]{:S(2)}) collective-permute-start(bf16[160,1280]{1,0:T(8,128)(2,1)S(1)} %collective-permute-done.3), channel_id=1, source_target_pairs={{0,28},{4,0},{8,4},{12,8},{16,12},{20,16},{24,20},{28,24},{1,29},{... | collective-permute-start | bytes 1228808 | tf_op jit(solution)/shard_map/ppermute | solution.py:64
  106.4 11.4 %collective-permute-start.5 = (bf16[160,1280]{1,0:T(8,128)(2,1)S(1)}, bf16[160,1280]{1,0:T(8,128)(2,1)S(1)}, u32[]{:S(2)}, u32[]{:S(2)}) collective-permute-start(bf16[160,1280]{1,0:T(8,128)(2,1)S(1)} %collective-permute-done.4), channel_id=1, source_target_pairs={{0,28},{4,0},{8,4},{12,8},{16,12},{20,16},{24,20},{28,24},{1,29},{... | collective-permute-start | bytes 1228808 | tf_op jit(solution)/shard_map/ppermute | solution.py:64
  117.8 22.2 %collective-permute-start.6 = (bf16[160,1280]{1,0:T(8,128)(2,1)S(1)}, bf16[160,1280]{1,0:T(8,128)(2,1)S(1)}, u32[]{:S(2)}, u32[]{:S(2)}) collective-permute-start(bf16[160,1280]{1,0:T(8,128)(2,1)S(1)} %collective-permute-done.5), channel_id=1, source_target_pairs={{0,28},{4,0},{8,4},{12,8},{16,12},{20,16},{24,20},{28,24},{1,29},{... | collective-permute-start | bytes 1228808 | tf_op jit(solution)/shard_map/ppermute | solution.py:64
  141.8 5.0 %copy-start.2 = (bf16[384,1280]{1,0:T(8,128)(2,1)}, bf16[384,1280]{1,0:T(8,128)(2,1)S(1)}, u32[]{:S(2)}) copy-start(bf16[384,1280]{1,0:T(8,128)(2,1)S(1)} %fusion.52) | copy-start | bytes 2949124
  183.2 2.9 copy-start.4
  186.1 82.5 %copy-start.3 = (bf16[384,1280]{1,0:T(8,128)(2,1)S(1)}, bf16[384,1280]{1,0:T(8,128)(2,1)}, u32[]{:S(2)}) copy-start(bf16[384,1280]{1,0:T(8,128)(2,1)} %copy-done.2) | copy-start | bytes 2949124
  268.6 8.9 %copy-start = (bf16[20,384,64]{2,1,0:T(8,128)(2,1)}, bf16[20,384,64]{2,1,0:T(8,128)(2,1)S(1)}, u32[]{:S(2)}) copy-start(bf16[20,384,64]{2,1,0:T(8,128)(2,1)S(1)} %get-tuple-element.436) | copy-start | bytes 2949124
Sparse Core Ops, SparseCore 0:
  10.2 93.3 all-gather.5
  105.7 73.7 all-gather.7
  181.1 53.9 all-gather.11
  237.2 61.2 all-gather.9
